TPU v7x, 512 devices: a whole 4x4x16 slice. The times are simulated.
512 devices in a mesh: seq: 64 (over z, y), tp: 8 (over x, core).
Axes of the slice: x: 4, y: 4, z: 16, core: 2. Of those that a mesh axis runs over, the one named last changes fastest.
Arguments:
- hidden: bfloat16 [384, 2048], P(None, 'seq'), may hold values from -12 to 12
- ln1_gain: float32 [2048], P('seq'), may hold values from 0.1 to 1.9
- wq: bfloat16 [2048, 2048], P('seq', 'tp'), may hold values from -0.125 to 0.125
- wk: bfloat16 [2048, 1024], P('seq', 'tp'), may hold values from -0.125 to 0.125
- wv: bfloat16 [2048, 1024], P('seq', 'tp'), may hold values from -0.125 to 0.125
- wg: bfloat16 [2048, 2048], P('seq', 'tp'), may hold values from -0.125 to 0.125
- q_gain: float32 [128], replicated, may hold values from 1 to 30
- key_gain: float32 [128], replicated, may hold values from 0.5 to 1.5
- wo: bfloat16 [2048, 2048], P('tp', 'seq'), may hold values from -0.5 to 0.5
- ln2_gain: float32 [2048], P('seq'), may hold values from 0.1 to 1.9
- w_gate: bfloat16 [2048, 6144], P('seq', 'tp'), may hold values from -0.125 to 0.125
- w_up: bfloat16 [2048, 6144], P('seq', 'tp'), may hold values from -0.125 to 0.125
- w_down: bfloat16 [6144, 2048], P('tp', 'seq'), may hold values from -0.078125 to 0.078125
- last_gain: float32 [2048], P('seq'), may hold values from 0.1 to 1.9
- head_weight: bfloat16 [2048, 131072], P(None, ('seq', 'tp')), may hold values from -0.125 to 0.125
- inv_temp: float32 [8], replicated, may hold values from 0.5 to 64
- key_cache: bfloat16 [8, 16384, 1024], P(None, 'seq', 'tp'), may hold values from -40 to 40
- value_cache: bfloat16 [8, 16384, 1024], P(None, 'seq', 'tp'), may hold values from -6 to 6
- lengths: int32 [8], replicated, may hold values from 1 to 16336
- parents: int32 [8, 48], replicated, may hold values from 0 to 46, as said below
- accepted: int32 [8], replicated, may hold values from 0 to 47
Outputs:
- logprobs: float32 [384, 131072], P(None, ('seq', 'tp'))
- next_hidden: bfloat16 [384, 2048], P(None, 'seq')
- updated_key_cache: bfloat16 [8, 16384, 1024], P(None, 'seq', 'tp')
- updated_value_cache: bfloat16 [8, 16384, 1024], P(None, 'seq', 'tp')
Inputs may be any that keep to these rules, and one draw needn't show every extreme that they name: parents[r, 0] = 0; for i >= 1, i - 4 <= parents[r, i] < i.
All inputs are finite; a program needn't handle non-finite values.
Results may differ from a plain program's by a relative error of at most 0.012.
Values may be sent and summed in bfloat16 or wider, within the bound.
No kernel may reach another device: no remote copies, remote signals or barrier semaphores. Data moves between devices by JAX's collectives and lax.ppermute only.
A program may use at most 128 MiB of HBM per device.

v0:
```python
import jax
import jax.numpy as jnp
from jax import lax
from jax.sharding import Mesh, PartitionSpec as P

EPSILON = 1e-06
ROPE_BASE = 1000000.0
NEGATIVE = -1e30
BF = jnp.bfloat16
F32 = jnp.float32


def ancestry(parents):
    node_count = parents.shape[-1]
    node_ids = jnp.arange(node_count, dtype=jnp.int32)
    reachable = (parents[..., :, None] == node_ids[None, :]).astype(BF)
    reachable = jnp.maximum(reachable, jnp.eye(node_count, dtype=BF))
    for turn in range((node_count - 1).bit_length()):
        reachable = jnp.minimum(
            jnp.einsum("rij,rjk->rik", reachable, reachable, preferred_element_type=F32), 1.0
        ).astype(BF)
    return reachable.astype(F32)


def head_norm(values, gain):
    meansq = jnp.mean(values * values, axis=-1, keepdims=True)
    return values * lax.rsqrt(meansq + EPSILON) * gain


def rotate(values, cosine, sine):
    half = values.shape[-1] // 2
    low, high = (values[..., :half], values[..., half:])
    return jnp.concatenate([low * cosine - high * sine, high * cosine + low * sine], axis=-1)


def swap(values, axis):
    return lax.all_to_all(values, axis, 0, 0, tiled=True)


def spread(values, axis, count):
    return swap(jnp.broadcast_to(values[None], (count,) + values.shape), axis)


def split2(values):
    high = values.astype(BF)
    low = (values - high.astype(F32)).astype(BF)
    return (high, low)


def split3(values):
    high = values.astype(BF)
    rest = values - high.astype(F32)
    mid = rest.astype(BF)
    low = (rest - mid.astype(F32)).astype(BF)
    return (high, mid, low)


def pack_state(peak, mass, weighted):
    count = peak.shape[0]
    mass_high, mass_low = split2(mass)
    stats = jnp.stack([peak.astype(BF), mass_high, mass_low], axis=1).reshape(count, 6, 24)
    stats = jnp.pad(stats, ((0, 0), (0, 2), (0, 104)))
    return jnp.concatenate([weighted.astype(BF).reshape(count, 48, 128), stats], axis=1)


def merge_state(packed):
    count = packed.shape[0]
    weighted = packed[:, :48].reshape(count, 2, 24, 128).astype(F32)
    stats = packed[:, 48:54, :24].astype(F32).reshape(count, 3, 2, 24)
    peaks, masses = (stats[:, 0], stats[:, 1] + stats[:, 2])
    peak = jnp.max(peaks, axis=0)
    factor = jnp.exp(peaks - peak)
    return (peak, jnp.sum(masses * factor, axis=0), jnp.sum(weighted * factor[..., None], axis=0))


def on_device(
    hidden,
    ln1_gain,
    wq,
    wk,
    wv,
    wg,
    q_gain,
    key_gain,
    wo,
    ln2_gain,
    w_gate,
    w_up,
    w_down,
    last_gain,
    head_weight,
    inv_temp,
    key_cache,
    value_cache,
    lengths,
    parents,
    accepted,
):
    z, y, x, c = (lax.axis_index(name) for name in ("z", "y", "x", "c"))
    seq = z * 4 + y
    requests, tree = parents.shape
    slot_count = key_cache.shape[1]
    width = 2048
    token = jnp.arange(384, dtype=jnp.int32)
    token_y = token // 6 % 4
    place = token_y * 128 + token // 24 * 6 + token % 6
    scatter = (place[:, None] == jnp.arange(512, dtype=jnp.int32)[None, :]).astype(BF)
    hidden_t = jnp.dot(hidden.T, scatter, preferred_element_type=F32).astype(BF)
    gains = jnp.stack(split3(ln1_gain) + split3(ln2_gain) + split3(last_gain), axis=1)
    gains = jnp.pad(gains, ((0, 0), (96, 128 - 96 - 9)))
    down_t, wo_t = (w_down.T, wo.T)
    pieces = []
    for part in range(4):
        pieces.append(
            jnp.concatenate(
                [
                    w_gate[:, part * 192 : part * 192 + 192],
                    w_up[:, part * 192 : part * 192 + 192],
                    down_t[:, part * 192 : part * 192 + 192],
                    wo_t[:, part * 64 : part * 64 + 64],
                    wq,
                    wk,
                    wv,
                    wg,
                    hidden_t[:, part * 128 : part * 128 + 128] + gains,
                ],
                axis=1,
            )
        )
    mine = swap(jnp.stack(pieces), "y").reshape(128, 1536)
    ffn = lax.all_gather(mine[:, :640], "z", axis=0, tiled=True)
    proj = mine[:, 640:1408]
    side = mine[:, 1408:]
    side_wide = side.astype(F32)
    ln1_row = side_wide[:, 96:97] + side_wide[:, 97:98] + side_wide[:, 98:99]
    scaled = (side_wide * ln1_row).astype(BF)
    partial = lax.dot_general(scaled, proj, (((0,), (0,)), ((), ())), preferred_element_type=F32)
    sent = jnp.concatenate([partial[:96].astype(BF), side.T[:96]], axis=1).reshape(16, 6, 896)
    got = swap(sent, "z")
    sums = jnp.sum(got[:, :, :768].astype(F32), axis=0)
    rows = got[:, :, 768:]
    rows_wide = rows.astype(F32)
    squares = jnp.sum(rows_wide * rows_wide, axis=(0, 2))
    sums = sums * lax.rsqrt(squares / width + EPSILON)[:, None]
    links = ancestry(parents)
    depth = jnp.sum((links > 0.5).astype(jnp.int32), axis=-1) - 1
    target = lengths[:, None] + depth
    my_places = lax.dynamic_slice(target.reshape(-1), (z * 24 + y * 6,), (6,))
    inverse = ROPE_BASE ** (-jnp.arange(64, dtype=F32) / 64)
    angles = my_places.astype(F32)[:, None] * inverse[None, :]
    cosine, sine = (jnp.cos(angles)[:, None, :], jnp.sin(angles)[:, None, :])
    query = rotate(head_norm(sums[:, :256].reshape(6, 2, 128), q_gain), cosine, sine) * 128 ** (
        -0.5
    )
    new_key = rotate(head_norm(sums[:, 256:384].reshape(6, 1, 128), key_gain), cosine, sine)
    outgate = jax.nn.sigmoid(sums[:, 512:])
    mine6 = jnp.concatenate(
        [query.reshape(6, 256), new_key.reshape(6, 128), sums[:, 384:512], outgate], axis=1
    ).astype(BF)
    gain_row = side[:, 99:105].T.reshape(1, 768)
    block = jnp.concatenate([mine6, gain_row, jnp.zeros((1, 768), BF)], axis=0)
    gathered = spread(block, "z", 16)
    gain_all = gathered[:, 6].reshape(16, 6, 128).astype(F32)
    ln2_all = gain_all[:, 0] + gain_all[:, 1] + gain_all[:, 2]
    last_all = gain_all[:, 3] + gain_all[:, 4] + gain_all[:, 5]
    tokens = spread(gathered[:, :6].reshape(96, 768), "y", 4).reshape(384, 768)
    order = token_y * 96 + token // 24 * 6 + token % 6
    gather = (order[:, None] == token[None, :]).astype(BF)
    tokens = jnp.dot(gather, tokens, preferred_element_type=F32).astype(BF)
    queries = tokens[:, :256].reshape(requests, tree, 2, 128)
    tree_keys = tokens[:, 256:384].reshape(requests, tree, 128)
    tree_values = tokens[:, 384:512].reshape(requests, tree, 128)
    gates = tokens[:, 512:]
    slot_ids = seq * slot_count + jnp.arange(slot_count, dtype=jnp.int32)
    valid_slot = (slot_ids[None, :] < lengths[:, None])[:, None, None, :]
    valid_node = ((links > 0.5) & (seq == 0))[:, None, :, :]
    scores = jnp.einsum("rigd,rcd->rgic", queries, key_cache, preferred_element_type=F32)
    tree_scores = jnp.einsum("rigd,rjd->rgij", queries, tree_keys, preferred_element_type=F32)
    peak = jnp.maximum(
        jnp.max(jnp.where(valid_slot, scores, NEGATIVE), axis=-1),
        jnp.max(jnp.where(valid_node, tree_scores, NEGATIVE), axis=-1),
    )
    peak = lax.reduce_precision(peak, 8, 7)
    weights = jnp.where(valid_slot, jnp.exp(scores - peak[..., None]), 0.0)
    tree_weights = jnp.where(valid_node, jnp.exp(tree_scores - peak[..., None]), 0.0)
    mass = jnp.sum(weights, axis=-1) + jnp.sum(tree_weights, axis=-1)
    weighted = jnp.einsum(
        "rgic,rcd->rgid", weights.astype(BF), value_cache, preferred_element_type=F32
    ) + jnp.einsum(
        "rgij,rjd->rgid", tree_weights.astype(BF), tree_values, preferred_element_type=F32
    )

    def by_z(values):
        split = values.reshape((requests, 2, 2, 24) + values.shape[3:])
        return jnp.swapaxes(split, 1, 2).reshape((16, 2, 24) + values.shape[3:])

    state = merge_state(swap(pack_state(by_z(peak), by_z(mass), by_z(weighted)), "z"))
    packed = pack_state(*(part[None] for part in state))[0]
    both = spread(jnp.concatenate([packed, rows.reshape(96, 128)], axis=0), "y", 4)
    peak, mass, weighted = merge_state(both[:, :56])
    my_gate = lax.dynamic_slice(gates, (z * 24, 0), (24, 256)).reshape(24, 2, 128)
    my_gate = jnp.swapaxes(my_gate, 0, 1).astype(F32)
    gated = (weighted / mass[..., None] * my_gate).astype(BF)
    gated = lax.dynamic_index_in_dim(gated, y // 2, 0, keepdims=False)
    gated = jnp.where(y % 2 == 0, gated[:, :64], gated[:, 64:])
    column = y * 4 + x
    hidden_mine = lax.dynamic_index_in_dim(
        both[:, 56:].reshape(4, 16, 6, 128), column, 1, keepdims=False
    ).reshape(24, 128)

    def reduce_columns(part):
        part = jnp.swapaxes(part.astype(BF).reshape(24, 16, 128), 0, 1)
        part = jnp.sum(swap(part, ("y", "x")).astype(F32), axis=0)
        return part + lax.ppermute(part, "c", [(0, 1), (1, 0)])

    attn = lax.dot_general(
        gated, ffn[:, 576:], (((1,), (1,)), ((), ())), preferred_element_type=F32
    )
    middle = (hidden_mine.astype(F32) + reduce_columns(attn)).astype(BF)
    middle_all = spread(middle, ("y", "x"), 16).astype(F32)
    squares_mid = jnp.sum(middle_all * middle_all, axis=(0, 2))
    scale_mid = lax.rsqrt(squares_mid / width + EPSILON)
    normed2 = (middle_all * scale_mid[None, :, None] * ln2_all[:, None, :]).astype(BF)
    normed2 = jnp.swapaxes(normed2, 0, 1).reshape(24, width)
    hidden_units = jnp.dot(normed2, ffn[:, :384], preferred_element_type=F32)
    activated = (jax.nn.silu(hidden_units[:, :192]) * hidden_units[:, 192:]).astype(BF)
    down = lax.dot_general(
        activated, ffn[:, 384:576], (((1,), (1,)), ((), ())), preferred_element_type=F32
    )
    following = (middle.astype(F32) + reduce_columns(down)).astype(BF)
    half = spread(following, "z", 16).reshape(384, 128)
    half = lax.dynamic_slice(half, (c * 192, 0), (192, 128))
    half = spread(spread(half, "y", 4), "x", 4)
    other = lax.ppermute(half, "c", [(0, 1), (1, 0)])
    full = jnp.stack([jnp.where(c == 0, half, other), jnp.where(c == 0, other, half)])
    own = lax.dynamic_slice(full, (0, z % 4, z // 4, 0, 0), (2, 1, 1, 192, 128)).reshape(384, 128)
    next_hidden = lax.dynamic_slice(own, (0, y * 32), (384, 32))
    full = jnp.transpose(full, (0, 3, 2, 1, 4)).reshape(384, width)
    wide = full.astype(F32)
    squares_last = jnp.sum(wide * wide, axis=1)
    normed3 = (
        wide * lax.rsqrt(squares_last / width + EPSILON)[:, None] * last_all.reshape(1, width)
    ).astype(BF)
    logits = jnp.dot(normed3, head_weight, preferred_element_type=F32)
    logits = logits * jnp.repeat(inv_temp, tree)[:, None]
    top = jnp.max(logits, axis=1)
    spot = top + jnp.log(jnp.sum(jnp.exp(logits - top[:, None]), axis=1))
    for axis, count in ((("y", "x", "c"), 32), ("z", 16)):
        spots = spread(spot.reshape(3, 128), axis, count)
        top = jnp.max(spots, axis=0)
        spot = top + jnp.log(jnp.sum(jnp.exp(spots - top), axis=0))
    logprobs = logits - spot.reshape(384, 1)
    accepted_rows = links[jnp.arange(requests), accepted]
    placed = (slot_ids[None, :, None] == target[:, None, :]).astype(F32) * accepted_rows[:, None, :]
    hits = (jnp.sum(placed, axis=2) > 0.5)[:, :, None]
    placed = placed.astype(BF)
    moved_keys = jnp.einsum("rca,rae->rce", placed, tree_keys, preferred_element_type=F32).astype(
        BF
    )
    moved_values = jnp.einsum(
        "rca,rae->rce", placed, tree_values, preferred_element_type=F32
    ).astype(BF)
    return (
        logprobs,
        next_hidden,
        jnp.where(hits, moved_keys, key_cache),
        jnp.where(hits, moved_values, value_cache),
    )


def solution(mesh):
    grid = Mesh(mesh.devices.reshape(16, 4, 4, 2), ("z", "y", "x", "c"))
    seq, tp = (("z", "y"), ("x", "c"))
    in_specs = (
        P(None, seq),
        P(seq),
        P(seq, tp),
        P(seq, tp),
        P(seq, tp),
        P(seq, tp),
        P(),
        P(),
        P(tp, seq),
        P(seq),
        P(seq, tp),
        P(seq, tp),
        P(tp, seq),
        P(seq),
        P(None, seq + tp),
        P(),
        P(None, seq, tp),
        P(None, seq, tp),
        P(),
        P(),
        P(),
    )
    out_specs = (P(None, seq + tp), P(None, seq), P(None, seq, tp), P(None, seq, tp))
    return jax.shard_map(
        on_device, mesh=grid, in_specs=in_specs, out_specs=out_specs, check_vma=False
    )
```

profile of v0, /device:TPU:1, one launch (start us, length us, event | category | flops | bytes accessed | tf_op | source)
XLA Modules:
  0.0 322.7 jit_solution(3381878387999184094)
XLA Ops:
  7.2 0.8 convert_bitcast_fusion.10
  8.3 0.7 convert_bitcast_fusion.7
  9.3 0.7 convert_bitcast_fusion.4
  10.4 0.9 fusion.142
  11.3 0.9 fusion.144
  12.1 1.0 fusion.19
  13.3 0.9 fusion.140
  14.3 0.9 concatenate.48
  15.1 0.9 concatenate.49
  16.0 0.9 concatenate.50
  16.9 0.9 concatenate.51
  17.7 0.8 pad_maximum_fusion.1
  18.5 5.0 %all-to-all-start = ((bf16[4,32,1536]{2,1,0:T(8,128)(2,1)}), bf16[4,32,1536]{2,1,0:T(8,128)(2,1)S(1)}, u32[]{:S(2)}, u32[]{:S(2)}) async-start(bf16[4,32,1536]{2,1,0:T(8,128)(2,1)} %pad_maximum_fusion.1), calls=%async_computation | async-start | bytes 786432 | tf_op jit(solution)/shard_map/all_to_all | solution.py:37
  24.5 1.1 fusion.72
  26.1 3.7 %all-to-all-done = bf16[4,32,1536]{2,1,0:T(8,128)(2,1)S(1)} async-done(((bf16[4,32,1536]{2,1,0:T(8,128)(2,1)}), bf16[4,32,1536]{2,1,0:T(8,128)(2,1)S(1)}, u32[]{:S(2)}, u32[]{:S(2)}) %all-to-all-start) | async-done | bytes 393248 | tf_op jit(solution)/shard_map/all_to_all | solution.py:37
  30.2 0.7 reshape.543
  30.9 15.6 %all-to-all-start.1 = ((bf16[16,6,896]{2,1,0:T(8,128)(2,1)}), bf16[16,6,896]{2,1,0:T(8,128)(2,1)S(1)}, u32[]{:S(2)}, u32[]{:S(2)}) async-start(bf16[16,6,896]{2,1,0:T(8,128)(2,1)} %reshape.543), calls=%async_computation.1 | async-start | bytes 458752 | tf_op jit(solution)/shard_map/all_to_all | solution.py:37
  46.9 12.2 %all-to-all-done.1 = bf16[16,6,896]{2,1,0:T(8,128)(2,1)S(1)} async-done(((bf16[16,6,896]{2,1,0:T(8,128)(2,1)}), bf16[16,6,896]{2,1,0:T(8,128)(2,1)S(1)}, u32[]{:S(2)}, u32[]{:S(2)}) %all-to-all-start.1) | async-done | bytes 172064 | tf_op jit(solution)/shard_map/all_to_all | solution.py:37
  60.2 0.7 broadcast_in_dim.72
  60.9 8.4 %all-to-all-start.2 = ((bf16[16,8,768]{2,1,0:T(8,128)(2,1)}), bf16[16,8,768]{2,1,0:T(8,128)(2,1)S(1)}, u32[]{:S(2)}, u32[]{:S(2)}) async-start(bf16[16,8,768]{2,1,0:T(8,128)(2,1)} %broadcast_in_dim.72), calls=%async_computation.2 | async-start | bytes 393216 | tf_op jit(solution)/shard_map/all_to_all | solution.py:37
  69.6 12.1 %all-to-all-done.2 = bf16[16,8,768]{2,1,0:T(8,128)(2,1)S(1)} async-done(((bf16[16,8,768]{2,1,0:T(8,128)(2,1)}), bf16[16,8,768]{2,1,0:T(8,128)(2,1)S(1)}, u32[]{:S(2)}, u32[]{:S(2)}) %all-to-all-start.2) | async-done | bytes 196640 | tf_op jit(solution)/shard_map/all_to_all | solution.py:37
  81.8 0.9 broadcast_in_dim.74
  82.6 3.6 %all-to-all-start.3 = ((bf16[4,96,768]{2,1,0:T(8,128)(2,1)}), bf16[4,96,768]{2,1,0:T(8,128)(2,1)S(1)}, u32[]{:S(2)}, u32[]{:S(2)}) async-start(bf16[4,96,768]{2,1,0:T(8,128)(2,1)} %broadcast_in_dim.74), calls=%async_computation.3 | async-start | bytes 1179648 | tf_op jit(solution)/shard_map/all_to_all | solution.py:37
  87.1 6.4 %all-to-all-done.3 = bf16[4,96,768]{2,1,0:T(8,128)(2,1)S(1)} async-done(((bf16[4,96,768]{2,1,0:T(8,128)(2,1)}), bf16[4,96,768]{2,1,0:T(8,128)(2,1)S(1)}, u32[]{:S(2)}, u32[]{:S(2)}) %all-to-all-start.3) | async-done | bytes 589856 | tf_op jit(solution)/shard_map/all_to_all | solution.py:37
  96.4 0.7 fusion.36
  97.1 7.2 %all-to-all-start.4 = ((bf16[16,56,128]{2,1,0:T(8,128)(2,1)}), bf16[16,56,128]{2,1,0:T(8,128)(2,1)S(1)}, u32[]{:S(2)}, u32[]{:S(2)}) async-start(bf16[16,56,128]{2,1,0:T(8,128)(2,1)} %fusion.36), calls=%async_computation.4 | async-start | bytes 458752 | tf_op jit(solution)/shard_map/all_to_all | solution.py:37
  104.4 13.2 %all-to-all-done.4 = bf16[16,56,128]{2,1,0:T(8,128)(2,1)S(1)} async-done(((bf16[16,56,128]{2,1,0:T(8,128)(2,1)}), bf16[16,56,128]{2,1,0:T(8,128)(2,1)S(1)}, u32[]{:S(2)}, u32[]{:S(2)}) %all-to-all-start.4) | async-done | bytes 229408 | tf_op jit(solution)/shard_map/all_to_all | solution.py:37
  118.2 0.7 broadcast_in_dim.80
  118.9 3.3 %all-to-all-start.5 = ((bf16[4,152,128]{2,1,0:T(8,128)(2,1)}), bf16[4,152,128]{2,1,0:T(8,128)(2,1)S(1)}, u32[]{:S(2)}, u32[]{:S(2)}) async-start(bf16[4,152,128]{2,1,0:T(8,128)(2,1)} %broadcast_in_dim.80), calls=%async_computation.5 | async-start | bytes 311296 | tf_op jit(solution)/shard_map/all_to_all | solution.py:37
  122.3 4.9 %all-to-all-done.5 = bf16[4,152,128]{2,1,0:T(8,128)(2,1)S(1)} async-done(((bf16[4,152,128]{2,1,0:T(8,128)(2,1)}), bf16[4,152,128]{2,1,0:T(8,128)(2,1)S(1)}, u32[]{:S(2)}, u32[]{:S(2)}) %all-to-all-start.5) | async-done | bytes 155680 | tf_op jit(solution)/shard_map/all_to_all | solution.py:37
  127.6 34.2 %all-gather.2.cloned.1.call-done = bf16[2048,640]{1,0:T(8,128)(2,1)} async-done(((bf16[128,640]{1,0:T(8,128)(2,1)}), bf16[2048,640]{1,0:T(8,128)(2,1)}) %all-gather.2.cloned.1.call-update) | async-done | bytes 2621456 | tf_op jit(solution)/shard_map/all_gather | solution.py:131
  161.8 1.4 fusion.17
  163.8 5.8 %all-to-all-start.6 = ((bf16[16,24,128]{2,1,0:T(8,128)(2,1)}), bf16[16,24,128]{2,1,0:T(8,128)(2,1)S(1)}, u32[]{:S(2)}, u32[]{:S(2)}) async-start(bf16[16,24,128]{2,1,0:T(8,128)(2,1)} %bitcast.189), calls=%async_computation.6 | async-start | bytes 196608 | tf_op jit(solution)/shard_map/all_to_all | solution.py:37
  169.9 6.4 %all-to-all-done.6 = bf16[16,24,128]{2,1,0:T(8,128)(2,1)S(1)} async-done(((bf16[16,24,128]{2,1,0:T(8,128)(2,1)}), bf16[16,24,128]{2,1,0:T(8,128)(2,1)S(1)}, u32[]{:S(2)}, u32[]{:S(2)}) %all-to-all-start.6) | async-done | bytes 98336 | tf_op jit(solution)/shard_map/all_to_all | solution.py:37
  176.3 12.0 %collective-permute-start = (f32[24,128]{1,0:T(8,128)S(1)}, f32[24,128]{1,0:T(8,128)S(1)}, u32[]{:S(2)}, u32[]{:S(2)}) collective-permute-start(f32[24,128]{1,0:T(8,128)S(1)} %convert_reduce_fusion.2), channel_id=1, source_target_pairs={{0,1},{1,0},{2,3},{3,2},{4,5},{5,4},{6,7},{7,6},{8,9},{9,8},{10,11... | collective-permute-start | bytes 36872 | tf_op jit(solution)/shard_map/ppermute | solution.py:214
  188.4 0.8 collective-permute-done
  189.8 3.5 %all-to-all-start.7 = ((bf16[16,24,128]{2,1,0:T(8,128)(2,1)}), bf16[16,24,128]{2,1,0:T(8,128)(2,1)S(1)}, u32[]{:S(2)}, u32[]{:S(2)}) async-start(bf16[16,24,128]{2,1,0:T(8,128)(2,1)} %broadcast_in_dim.81), calls=%async_computation.7 | async-start | bytes 196608 | tf_op jit(solution)/shard_map/all_to_all | solution.py:37
  193.4 6.6 %all-to-all-done.7 = bf16[16,24,128]{2,1,0:T(8,128)(2,1)S(1)} async-done(((bf16[16,24,128]{2,1,0:T(8,128)(2,1)}), bf16[16,24,128]{2,1,0:T(8,128)(2,1)S(1)}, u32[]{:S(2)}, u32[]{:S(2)}) %all-to-all-start.7) | async-done | bytes 98336 | tf_op jit(solution)/shard_map/all_to_all | solution.py:37
  200.1 1.8 fusion.2
  201.9 1.6 fusion.18
  203.5 9.8 %all_to_all.70 = bf16[16,24,128]{2,1,0:T(8,128)(2,1)S(1)} all-to-all(bf16[16,24,128]{2,1,0:T(8,128)(2,1)S(1)} %bitcast.208), channel_id=1, replica_groups=mesh['z'=16,'y'=4,'x'=4,'c'=2] {'y','x'}, dimensions={0} | all-to-all | bytes 196608 | tf_op jit(solution)/shard_map/all_to_all | solution.py:37
  213.4 4.5 %collective-permute-start.1 = (f32[24,128]{1,0:T(8,128)S(1)}, f32[24,128]{1,0:T(8,128)S(1)}, u32[]{:S(2)}, u32[]{:S(2)}) collective-permute-start(f32[24,128]{1,0:T(8,128)S(1)} %convert_reduce_fusion.1), channel_id=1, source_target_pairs={{0,1},{1,0},{2,3},{3,2},{4,5},{5,4},{6,7},{7,6},{8,9},{9,8},{10,11... | collective-permute-start | bytes 36872 | tf_op jit(solution)/shard_map/ppermute | solution.py:214
  217.9 0.8 collective-permute-done.1
  219.4 6.5 %all-to-all-start.9 = ((bf16[16,24,128]{2,1,0:T(8,128)(2,1)}), bf16[16,24,128]{2,1,0:T(8,128)(2,1)S(1)}, u32[]{:S(2)}, u32[]{:S(2)}) async-start(bf16[16,24,128]{2,1,0:T(8,128)(2,1)} %broadcast_in_dim.82), calls=%async_computation.9 | async-start | bytes 196608 | tf_op jit(solution)/shard_map/all_to_all | solution.py:37
  225.9 11.9 %all-to-all-done.9 = bf16[16,24,128]{2,1,0:T(8,128)(2,1)S(1)} async-done(((bf16[16,24,128]{2,1,0:T(8,128)(2,1)}), bf16[16,24,128]{2,1,0:T(8,128)(2,1)S(1)}, u32[]{:S(2)}, u32[]{:S(2)}) %all-to-all-start.9) | async-done | bytes 98336 | tf_op jit(solution)/shard_map/all_to_all | solution.py:37
  237.8 7.5 %all_to_all.71 = bf16[4,192,128]{2,1,0:T(8,128)(2,1)S(1)} all-to-all(bf16[4,192,128]{2,1,0:T(8,128)(2,1)S(1)} %broadcast_in_dim.83), channel_id=1, replica_groups=mesh['z'=16,'y'=4,'x'=4,'c'=2] {'y'}, dimensions={0} | all-to-all | bytes 393216 | tf_op jit(solution)/shard_map/all_to_all | solution.py:37
  245.3 1.0 broadcast_in_dim.84
  246.4 3.5 %all-to-all-start.11 = ((bf16[4,4,192,128]{3,2,1,0:T(8,128)(2,1)}), bf16[4,4,192,128]{3,2,1,0:T(8,128)(2,1)S(1)}, u32[]{:S(2)}, u32[]{:S(2)}) async-start(bf16[4,4,192,128]{3,2,1,0:T(8,128)(2,1)} %broadcast_in_dim.84), calls=%async_computation.11 | async-start | bytes 1572864 | tf_op jit(solution)/shard_map/all_to_all | solution.py:37
  249.9 1.5 gather_fusion
  251.4 6.8 %all-to-all-done.11 = bf16[4,4,192,128]{3,2,1,0:T(8,128)(2,1)S(1)} async-done(((bf16[4,4,192,128]{3,2,1,0:T(8,128)(2,1)}), bf16[4,4,192,128]{3,2,1,0:T(8,128)(2,1)S(1)}, u32[]{:S(2)}, u32[]{:S(2)}) %all-to-all-start.11) | async-done | bytes 786464 | tf_op jit(solution)/shard_map/all_to_all | solution.py:37
  258.2 7.0 %collective-permute-start.2 = (bf16[4,4,192,128]{3,2,1,0:T(8,128)(2,1)S(1)}, bf16[4,4,192,128]{3,2,1,0:T(8,128)(2,1)}, u32[]{:S(2)}, u32[]{:S(2)}) collective-permute-start(bf16[4,4,192,128]{3,2,1,0:T(8,128)(2,1)S(1)} %all-to-all-done.11), channel_id=1, source_target_pairs={{0,1},{1,0},{2,3},{3,2},{4,5},{5,4},{6,7},{7,6},{8,9},{9,8},{10,11... | collective-permute-start | bytes 2359304 | tf_op jit(solution)/shard_map/ppermute | solution.py:234
  265.6 1.7 fusion.6
  267.3 1.6 fusion.7
  268.9 1.2 select_bitcast_fusion.1
  270.5 1.9 convert_bitcast_fusion
  272.5 5.6 %copy.190 = f32[2,192,4,4,128]{4,3,2,1,0:T(4,128)} copy(f32[2,192,4,4,128]{4,1,2,3,0:T(8,128)} %convert_bitcast_fusion) | data formatting | bytes 6291456 | tf_op jit(solution)/shard_map/convert_element_type | solution.py:239
  278.1 5.1 %reshape.571 = f32[384,2048]{1,0:T(8,128)} reshape(f32[2,192,4,4,128]{4,3,2,1,0:T(4,128)} %copy.190) | data formatting | bytes 6291456 | tf_op jit(solution)/shard_map/convert_element_type | solution.py:239
  283.2 2.7 fusion.148
  286.7 3.6 %all-to-all-start.12 = ((f32[32,3,128]{2,1,0:T(4,128)}), f32[32,3,128]{2,1,0:T(4,128)S(1)}, u32[]{:S(2)}, u32[]{:S(2)}) async-start(f32[32,3,128]{2,1,0:T(4,128)} %broadcast_in_dim.86), calls=%async_computation.12 | async-start | bytes 131072 | tf_op jit(solution)/shard_map/all_to_all | solution.py:37
  290.4 7.3 %all-to-all-done.12 = f32[32,3,128]{2,1,0:T(4,128)S(1)} async-done(((f32[32,3,128]{2,1,0:T(4,128)}), f32[32,3,128]{2,1,0:T(4,128)S(1)}, u32[]{:S(2)}, u32[]{:S(2)}) %all-to-all-start.12) | async-done | bytes 49184 | tf_op jit(solution)/shard_map/all_to_all | solution.py:37
  298.4 4.9 %all-to-all-start.13 = ((f32[16,3,128]{2,1,0:T(4,128)}), f32[16,3,128]{2,1,0:T(4,128)S(1)}, u32[]{:S(2)}, u32[]{:S(2)}) async-start(f32[16,3,128]{2,1,0:T(4,128)} %broadcast_in_dim.87), calls=%async_computation.13 | async-start | bytes 65536 | tf_op jit(solution)/shard_map/all_to_all | solution.py:37
  303.4 0.7 copy.196
  304.1 10.7 %all-to-all-done.13 = f32[16,3,128]{2,1,0:T(4,128)S(1)} async-done(((f32[16,3,128]{2,1,0:T(4,128)}), f32[16,3,128]{2,1,0:T(4,128)S(1)}, u32[]{:S(2)}, u32[]{:S(2)}) %all-to-all-start.13) | async-done | bytes 24608 | tf_op jit(solution)/shard_map/all_to_all | solution.py:37
  314.9 0.9 copy.195
  (174 shorter events, 14.2 us)
Async XLA Ops:
  7.2 276.0 %copy-start = (bf16[2048,256]{1,0:T(8,128)(2,1)S(1)}, bf16[2048,256]{1,0:T(8,128)(2,1)}, u32[]{:S(2)}) copy-start(bf16[2048,256]{1,0:T(8,128)(2,1)} %param.35) | copy-start | bytes 3145732
  7.2 16.4 %copy-start.7 = (s32[8,48]{1,0:T(8,128)S(1)}, s32[8,48]{1,0:T(8,128)}, u32[]{:S(2)}) copy-start(s32[8,48]{1,0:T(8,128)} %param.40) | copy-start | bytes 4612
  7.2 18.6 %copy-start.3 = (s32[8]{0:T(128)S(1)}, s32[8]{0:T(128)}, u32[]{:S(2)}) copy-start(s32[8]{0:T(128)} %param.39) | copy-start | bytes 100
  17.7 41.9 %copy-start.4 = (f32[128]{0:T(128)S(1)}, f32[128]{0:T(128)}, u32[]{:S(2)}) copy-start(f32[128]{0:T(128)} %param.27) | copy-start | bytes 1540
  17.7 42.2 %copy-start.5 = (f32[128]{0:T(128)S(1)}, f32[128]{0:T(128)}, u32[]{:S(2)}) copy-start(f32[128]{0:T(128)} %param.28) | copy-start | bytes 1540
  18.5 11.2 %all-to-all-start = ((bf16[4,32,1536]{2,1,0:T(8,128)(2,1)}), bf16[4,32,1536]{2,1,0:T(8,128)(2,1)S(1)}, u32[]{:S(2)}, u32[]{:S(2)}) async-start(bf16[4,32,1536]{2,1,0:T(8,128)(2,1)} %pad_maximum_fusion.1), calls=%async_computation | async-start | bytes 786432 | tf_op jit(solution)/shard_map/all_to_all | solution.py:37
  30.9 28.2 %all-to-all-start.1 = ((bf16[16,6,896]{2,1,0:T(8,128)(2,1)}), bf16[16,6,896]{2,1,0:T(8,128)(2,1)S(1)}, u32[]{:S(2)}, u32[]{:S(2)}) async-start(bf16[16,6,896]{2,1,0:T(8,128)(2,1)} %reshape.543), calls=%async_computation.1 | async-start | bytes 458752 | tf_op jit(solution)/shard_map/all_to_all | solution.py:37
  60.9 20.8 %all-to-all-start.2 = ((bf16[16,8,768]{2,1,0:T(8,128)(2,1)}), bf16[16,8,768]{2,1,0:T(8,128)(2,1)S(1)}, u32[]{:S(2)}, u32[]{:S(2)}) async-start(bf16[16,8,768]{2,1,0:T(8,128)(2,1)} %broadcast_in_dim.72), calls=%async_computation.2 | async-start | bytes 393216 | tf_op jit(solution)/shard_map/all_to_all | solution.py:37
  82.6 11.9 %copy-start.1 = (bf16[8,256,128]{2,1,0:T(8,128)(2,1)S(1)}, bf16[8,256,128]{2,1,0:T(8,128)(2,1)}, u32[]{:S(2)}) copy-start(bf16[8,256,128]{2,1,0:T(8,128)(2,1)} %param.37) | copy-start | bytes 1572868
  82.6 10.9 %all-to-all-start.3 = ((bf16[4,96,768]{2,1,0:T(8,128)(2,1)}), bf16[4,96,768]{2,1,0:T(8,128)(2,1)S(1)}, u32[]{:S(2)}, u32[]{:S(2)}) async-start(bf16[4,96,768]{2,1,0:T(8,128)(2,1)} %broadcast_in_dim.74), calls=%async_computation.3 | async-start | bytes 1179648 | tf_op jit(solution)/shard_map/all_to_all | solution.py:37
  86.2 75.6 %all-gather.2.cloned.1.call-start = ((), (), s32[]{:S(2)}) async-start(), calls=%async_computation.14 | async-start | bytes 2785280 | tf_op jit(solution)/shard_map/all_gather | solution.py:131
  94.0 1.7 copy-start.2
  97.1 20.5 %all-to-all-start.4 = ((bf16[16,56,128]{2,1,0:T(8,128)(2,1)}), bf16[16,56,128]{2,1,0:T(8,128)(2,1)S(1)}, u32[]{:S(2)}, u32[]{:S(2)}) async-start(bf16[16,56,128]{2,1,0:T(8,128)(2,1)} %fusion.36), calls=%async_computation.4 | async-start | bytes 458752 | tf_op jit(solution)/shard_map/all_to_all | solution.py:37
  118.9 8.3 %all-to-all-start.5 = ((bf16[4,152,128]{2,1,0:T(8,128)(2,1)}), bf16[4,152,128]{2,1,0:T(8,128)(2,1)S(1)}, u32[]{:S(2)}, u32[]{:S(2)}) async-start(bf16[4,152,128]{2,1,0:T(8,128)(2,1)} %broadcast_in_dim.80), calls=%async_computation.5 | async-start | bytes 311296 | tf_op jit(solution)/shard_map/all_to_all | solution.py:37
  163.8 12.4 %all-to-all-start.6 = ((bf16[16,24,128]{2,1,0:T(8,128)(2,1)}), bf16[16,24,128]{2,1,0:T(8,128)(2,1)S(1)}, u32[]{:S(2)}, u32[]{:S(2)}) async-start(bf16[16,24,128]{2,1,0:T(8,128)(2,1)} %bitcast.189), calls=%async_computation.6 | async-start | bytes 196608 | tf_op jit(solution)/shard_map/all_to_all | solution.py:37
  176.3 12.8 %collective-permute-start = (f32[24,128]{1,0:T(8,128)S(1)}, f32[24,128]{1,0:T(8,128)S(1)}, u32[]{:S(2)}, u32[]{:S(2)}) collective-permute-start(f32[24,128]{1,0:T(8,128)S(1)} %convert_reduce_fusion.2), channel_id=1, source_target_pairs={{0,1},{1,0},{2,3},{3,2},{4,5},{5,4},{6,7},{7,6},{8,9},{9,8},{10,11... | collective-permute-start | bytes 36872 | tf_op jit(solution)/shard_map/ppermute | solution.py:214
  189.8 10.1 %all-to-all-start.7 = ((bf16[16,24,128]{2,1,0:T(8,128)(2,1)}), bf16[16,24,128]{2,1,0:T(8,128)(2,1)S(1)}, u32[]{:S(2)}, u32[]{:S(2)}) async-start(bf16[16,24,128]{2,1,0:T(8,128)(2,1)} %broadcast_in_dim.81), calls=%async_computation.7 | async-start | bytes 196608 | tf_op jit(solution)/shard_map/all_to_all | solution.py:37
  201.9 48.0 %copy-start.8 = (s32[8]{0:T(128)S(1)}, s32[8]{0:T(128)}, u32[]{:S(2)}) copy-start(s32[8]{0:T(128)} %param.41) | copy-start | bytes 100
  201.9 63.6 %copy-start.6 = (f32[8]{0:T(128)S(1)}, f32[8]{0:T(128)}, u32[]{:S(2)}) copy-start(f32[8]{0:T(128)} %param.36) | copy-start | bytes 100
  213.4 5.4 %collective-permute-start.1 = (f32[24,128]{1,0:T(8,128)S(1)}, f32[24,128]{1,0:T(8,128)S(1)}, u32[]{:S(2)}, u32[]{:S(2)}) collective-permute-start(f32[24,128]{1,0:T(8,128)S(1)} %convert_reduce_fusion.1), channel_id=1, source_target_pairs={{0,1},{1,0},{2,3},{3,2},{4,5},{5,4},{6,7},{7,6},{8,9},{9,8},{10,11... | collective-permute-start | bytes 36872 | tf_op jit(solution)/shard_map/ppermute | solution.py:214
  219.4 18.4 %all-to-all-start.9 = ((bf16[16,24,128]{2,1,0:T(8,128)(2,1)}), bf16[16,24,128]{2,1,0:T(8,128)(2,1)S(1)}, u32[]{:S(2)}, u32[]{:S(2)}) async-start(bf16[16,24,128]{2,1,0:T(8,128)(2,1)} %broadcast_in_dim.82), calls=%async_computation.9 | async-start | bytes 196608 | tf_op jit(solution)/shard_map/all_to_all | solution.py:37
  246.4 11.8 %all-to-all-start.11 = ((bf16[4,4,192,128]{3,2,1,0:T(8,128)(2,1)}), bf16[4,4,192,128]{3,2,1,0:T(8,128)(2,1)S(1)}, u32[]{:S(2)}, u32[]{:S(2)}) async-start(bf16[4,4,192,128]{3,2,1,0:T(8,128)(2,1)} %broadcast_in_dim.84), calls=%async_computation.11 | async-start | bytes 1572864 | tf_op jit(solution)/shard_map/all_to_all | solution.py:37
  258.2 10.7 %collective-permute-start.2 = (bf16[4,4,192,128]{3,2,1,0:T(8,128)(2,1)S(1)}, bf16[4,4,192,128]{3,2,1,0:T(8,128)(2,1)}, u32[]{:S(2)}, u32[]{:S(2)}) collective-permute-start(bf16[4,4,192,128]{3,2,1,0:T(8,128)(2,1)S(1)} %all-to-all-done.11), channel_id=1, source_target_pairs={{0,1},{1,0},{2,3},{3,2},{4,5},{5,4},{6,7},{7,6},{8,9},{9,8},{10,11... | collective-permute-start | bytes 2359304 | tf_op jit(solution)/shard_map/ppermute | solution.py:234
  286.7 11.0 %all-to-all-start.12 = ((f32[32,3,128]{2,1,0:T(4,128)}), f32[32,3,128]{2,1,0:T(4,128)S(1)}, u32[]{:S(2)}, u32[]{:S(2)}) async-start(f32[32,3,128]{2,1,0:T(4,128)} %broadcast_in_dim.86), calls=%async_computation.12 | async-start | bytes 131072 | tf_op jit(solution)/shard_map/all_to_all | solution.py:37
  298.4 16.4 %all-to-all-start.13 = ((f32[16,3,128]{2,1,0:T(4,128)}), f32[16,3,128]{2,1,0:T(4,128)S(1)}, u32[]{:S(2)}, u32[]{:S(2)}) async-start(f32[16,3,128]{2,1,0:T(4,128)} %broadcast_in_dim.87), calls=%async_computation.13 | async-start | bytes 65536 | tf_op jit(solution)/shard_map/all_to_all | solution.py:37
Sparse Core Ops, SparseCore 0:
  89.7 72.0 all-gather.1
where the time goes:
time: 325 us; the launch traced here: 323 us
  waiting for transfers between devices  138 us (42%)
  starting transfers between devices  94.6 us (29%)
  local copies, waits for them, and re-layouts  30.7 us (9%)
  blocking collectives  17.3 us (5%)
  matrix products  15.9 us (5%)
  between operations  14.9 us (5%)
  other arithmetic  11.1 us (3%)
    all_to_all x12, waiting for transfers between devices, swap(): return lax.all_to_all(values, axis, 0, 0, tiled=True)  102 us
    all_to_all x12, starting transfers between devices, swap(): return lax.all_to_all(values, axis, 0, 0, tiled=True)  71 us
    all_gather x1, waiting for transfers between devices, on_device(): ffn = lax.all_gather(mine[:, :640], 'z', axis=0, tiled=True)  34.2 us
    all_to_all x2, blocking collectives, swap(): return lax.all_to_all(values, axis, 0, 0, tiled=True)  17.3 us
    ppermute x2, starting transfers between devices, reduce_columns(): return part + lax.ppermute(part, 'c', [(0, 1), (1, 0)])  16.6 us
    convert_element_type x2, local copies, waits for them, and re-layouts, on_device(): wide = full.astype(F32)  10.6 us
    ppermute x1, starting transfers between devices, on_device(): other = lax.ppermute(half, 'c', [(0, 1), (1, 0)])  7.02 us
  transfers between devices with their start and end apart: 16, of which 15 were waited for; matrix products, arithmetic and copies ran while one was open for 5% of the time, Pallas kernels for 0%

commit v1 on v0

--- a/solution.py
+++ b/solution.py
@@ -128,7 +128,11 @@
             )
         )
     mine = swap(jnp.stack(pieces), "y").reshape(128, 1536)
-    ffn = lax.all_gather(mine[:, :640], "z", axis=0, tiled=True)
+    part_2 = mine[:, :640]
+    size = lax.axis_size("z")
+    parts = jnp.stack([part_2 for _ in range(size)])
+    parts = lax.all_to_all(parts, "z", split_axis=0, concat_axis=0)
+    ffn = jnp.concatenate(parts, axis=0)
     proj = mine[:, 640:1408]
     side = mine[:, 1408:]
     side_wide = side.astype(F32)

time: 325 us -> 397 us (1.22)
  waiting for transfers between devices: 138 us -> 216 us
  between operations: 14.9 us -> 1.68 us
    all_to_all x0 -> x1, waiting for transfers between devices: none -> 113 us  [on_device(): parts = lax.all_to_all(parts, 'z', split_axis=0, concat_axis=0)]
    all_gather x1 -> x0, waiting for transfers between devices: 34.2 us -> none  [on_device(): ffn = lax.all_gather(mine[:, :640], 'z', axis=0, tiled=True)]
    all_to_all x0 -> x1, starting transfers between devices: none -> 7.54 us  [on_device(): parts = lax.all_to_all(parts, 'z', split_axis=0, concat_axis=0)]
    ppermute x2, starting transfers between devices: 16.6 us -> 9.47 us  [reduce_columns(): return part + lax.ppermute(part, 'c', [(0, 1), (1, 0)])]
  transfers between devices with their start and end apart: 16 -> 16, of which waited for: 15 -> 15; matrix products, arithmetic and copies ran while one was open for 5% -> 3% of each run, Pallas kernels for 0% -> 0%
where the time goes in v1:
time: 397 us; the launch traced here: 395 us
  waiting for transfers between devices  216 us (54%)
  starting transfers between devices  97.5 us (25%)
  local copies, waits for them, and re-layouts  33.2 us (8%)
  blocking collectives  17.3 us (4%)
  matrix products  16.6 us (4%)
  other arithmetic  13.1 us (3%)
    all_to_all x1, waiting for transfers between devices, on_device(): parts = lax.all_to_all(parts, 'z', split_axis=0, concat_axis=0)  113 us
    all_to_all x12, waiting for transfers between devices, swap(): return lax.all_to_all(values, axis, 0, 0, tiled=True)  101 us
    all_to_all x12, starting transfers between devices, swap(): return lax.all_to_all(values, axis, 0, 0, tiled=True)  73.5 us
    all_to_all x2, blocking collectives, swap(): return lax.all_to_all(values, axis, 0, 0, tiled=True)  17.3 us
    convert_element_type x2, local copies, waits for them, and re-layouts, on_device(): wide = full.astype(F32)  10.6 us
    ppermute x2, starting transfers between devices, reduce_columns(): return part + lax.ppermute(part, 'c', [(0, 1), (1, 0)])  9.47 us
  transfers between devices with their start and end apart: 16, of which 15 were waited for; matrix products, arithmetic and copies ran while one was open for 3% of the time, Pallas kernels for 0%

profile of v1, /device:TPU:1, one launch (start us, length us, event | category | flops | bytes accessed | tf_op | source)
XLA Modules:
  0.0 395.3 jit_solution(2179890351351210442)
XLA Ops:
  0.7 0.8 convert_bitcast_fusion.10
  1.7 0.7 convert_bitcast_fusion.7
  2.8 0.7 convert_bitcast_fusion.4
  3.8 0.9 fusion.142
  4.7 0.9 fusion.144
  5.6 1.0 fusion.19
  6.8 0.9 fusion.140
  7.8 0.9 concatenate.48
  8.6 0.9 concatenate.49
  9.5 0.9 concatenate.50
  10.3 0.9 concatenate.51
  11.2 0.8 pad_maximum_fusion.1
  12.0 5.0 %all-to-all-start = ((bf16[4,32,1536]{2,1,0:T(8,128)(2,1)}), bf16[4,32,1536]{2,1,0:T(8,128)(2,1)S(1)}, u32[]{:S(2)}, u32[]{:S(2)}) async-start(bf16[4,32,1536]{2,1,0:T(8,128)(2,1)} %pad_maximum_fusion.1), calls=%async_computation | async-start | bytes 786432 | tf_op jit(solution)/shard_map/all_to_all | solution.py:37
  18.0 1.1 fusion.72
  19.5 3.7 all-to-all-done
  23.7 0.7 reshape.548
  24.4 15.5 %all-to-all-start.1 = ((bf16[16,6,896]{2,1,0:T(8,128)(2,1)}), bf16[16,6,896]{2,1,0:T(8,128)(2,1)S(1)}, u32[]{:S(2)}, u32[]{:S(2)}) async-start(bf16[16,6,896]{2,1,0:T(8,128)(2,1)} %reshape.548), calls=%async_computation.1 | async-start | bytes 458752 | tf_op jit(solution)/shard_map/all_to_all | solution.py:37
  40.4 12.2 %all-to-all-done.1 = bf16[16,6,896]{2,1,0:T(8,128)(2,1)S(1)} async-done(((bf16[16,6,896]{2,1,0:T(8,128)(2,1)}), bf16[16,6,896]{2,1,0:T(8,128)(2,1)S(1)}, u32[]{:S(2)}, u32[]{:S(2)}) %all-to-all-start.1) | async-done | bytes 172064 | tf_op jit(solution)/shard_map/all_to_all | solution.py:37
  54.4 8.4 %all-to-all-start.2 = ((bf16[16,8,768]{2,1,0:T(8,128)(2,1)}), bf16[16,8,768]{2,1,0:T(8,128)(2,1)S(1)}, u32[]{:S(2)}, u32[]{:S(2)}) async-start(bf16[16,8,768]{2,1,0:T(8,128)(2,1)} %broadcast_in_dim.72), calls=%async_computation.2 | async-start | bytes 393216 | tf_op jit(solution)/shard_map/all_to_all | solution.py:37
  63.0 12.1 %all-to-all-done.2 = bf16[16,8,768]{2,1,0:T(8,128)(2,1)S(1)} async-done(((bf16[16,8,768]{2,1,0:T(8,128)(2,1)}), bf16[16,8,768]{2,1,0:T(8,128)(2,1)S(1)}, u32[]{:S(2)}, u32[]{:S(2)}) %all-to-all-start.2) | async-done | bytes 196640 | tf_op jit(solution)/shard_map/all_to_all | solution.py:37
  75.2 0.8 broadcast_in_dim.74
  76.1 3.5 all-to-all-start.3
  80.8 6.0 %all-to-all-done.3 = bf16[4,96,768]{2,1,0:T(8,128)(2,1)S(1)} async-done(((bf16[4,96,768]{2,1,0:T(8,128)(2,1)}), bf16[4,96,768]{2,1,0:T(8,128)(2,1)S(1)}, u32[]{:S(2)}, u32[]{:S(2)}) %all-to-all-start.3) | async-done | bytes 589856 | tf_op jit(solution)/shard_map/all_to_all | solution.py:37
  88.5 1.1 select_reduce_fusion
  89.6 1.0 fusion.21
  92.5 7.2 %all-to-all-start.4 = ((bf16[16,56,128]{2,1,0:T(8,128)(2,1)}), bf16[16,56,128]{2,1,0:T(8,128)(2,1)S(1)}, u32[]{:S(2)}, u32[]{:S(2)}) async-start(bf16[16,56,128]{2,1,0:T(8,128)(2,1)} %fusion.36), calls=%async_computation.4 | async-start | bytes 458752 | tf_op jit(solution)/shard_map/all_to_all | solution.py:37
  99.8 12.5 %all-to-all-done.4 = bf16[16,56,128]{2,1,0:T(8,128)(2,1)S(1)} async-done(((bf16[16,56,128]{2,1,0:T(8,128)(2,1)}), bf16[16,56,128]{2,1,0:T(8,128)(2,1)S(1)}, u32[]{:S(2)}, u32[]{:S(2)}) %all-to-all-start.4) | async-done | bytes 229408 | tf_op jit(solution)/shard_map/all_to_all | solution.py:37
  113.5 3.3 all-to-all-start.5
  116.9 4.9 %all-to-all-done.5 = bf16[4,152,128]{2,1,0:T(8,128)(2,1)S(1)} async-done(((bf16[4,152,128]{2,1,0:T(8,128)(2,1)}), bf16[4,152,128]{2,1,0:T(8,128)(2,1)S(1)}, u32[]{:S(2)}, u32[]{:S(2)}) %all-to-all-start.5) | async-done | bytes 155680 | tf_op jit(solution)/shard_map/all_to_all | solution.py:37
  121.8 1.8 stack.102
  123.6 7.5 %all-to-all-start.6 = ((bf16[16,128,640]{2,1,0:T(8,128)(2,1)}), bf16[16,128,640]{2,1,0:T(8,128)(2,1)}, u32[]{:S(2)}, u32[]{:S(2)}) async-start(bf16[16,128,640]{2,1,0:T(8,128)(2,1)} %stack.102), calls=%async_computation.6 | async-start | bytes 5242880 | tf_op jit(solution)/shard_map/all_to_all | solution.py:134
  132.4 113.2 %all-to-all-done.6 = bf16[16,128,640]{2,1,0:T(8,128)(2,1)} async-done(((bf16[16,128,640]{2,1,0:T(8,128)(2,1)}), bf16[16,128,640]{2,1,0:T(8,128)(2,1)}, u32[]{:S(2)}, u32[]{:S(2)}) %all-to-all-start.6) | async-done | bytes 2621472 | tf_op jit(solution)/shard_map/all_to_all | solution.py:134
  245.5 1.4 fusion.17
  247.6 4.8 %all-to-all-start.7 = ((bf16[16,24,128]{2,1,0:T(8,128)(2,1)}), bf16[16,24,128]{2,1,0:T(8,128)(2,1)S(1)}, u32[]{:S(2)}, u32[]{:S(2)}) async-start(bf16[16,24,128]{2,1,0:T(8,128)(2,1)} %bitcast.190), calls=%async_computation.7 | async-start | bytes 196608 | tf_op jit(solution)/shard_map/all_to_all | solution.py:37
  252.6 6.4 %all-to-all-done.7 = bf16[16,24,128]{2,1,0:T(8,128)(2,1)S(1)} async-done(((bf16[16,24,128]{2,1,0:T(8,128)(2,1)}), bf16[16,24,128]{2,1,0:T(8,128)(2,1)S(1)}, u32[]{:S(2)}, u32[]{:S(2)}) %all-to-all-start.7) | async-done | bytes 98336 | tf_op jit(solution)/shard_map/all_to_all | solution.py:37
  259.0 4.8 %collective-permute-start = (f32[24,128]{1,0:T(8,128)S(1)}, f32[24,128]{1,0:T(8,128)S(1)}, u32[]{:S(2)}, u32[]{:S(2)}) collective-permute-start(f32[24,128]{1,0:T(8,128)S(1)} %convert_reduce_fusion.2), channel_id=1, source_target_pairs={{0,1},{1,0},{2,3},{3,2},{4,5},{5,4},{6,7},{7,6},{8,9},{9,8},{10,11... | collective-permute-start | bytes 36872 | tf_op jit(solution)/shard_map/ppermute | solution.py:218
  263.9 0.8 collective-permute-done
  265.3 3.5 all-to-all-start.8
  268.9 6.6 %all-to-all-done.8 = bf16[16,24,128]{2,1,0:T(8,128)(2,1)S(1)} async-done(((bf16[16,24,128]{2,1,0:T(8,128)(2,1)}), bf16[16,24,128]{2,1,0:T(8,128)(2,1)S(1)}, u32[]{:S(2)}, u32[]{:S(2)}) %all-to-all-start.8) | async-done | bytes 98336 | tf_op jit(solution)/shard_map/all_to_all | solution.py:37
  275.6 1.8 fusion.2
  277.4 1.7 fusion.18
  279.1 9.8 %all_to_all.75 = bf16[16,24,128]{2,1,0:T(8,128)(2,1)S(1)} all-to-all(bf16[16,24,128]{2,1,0:T(8,128)(2,1)S(1)} %bitcast.209), channel_id=1, replica_groups=mesh['z'=16,'y'=4,'x'=4,'c'=2] {'y','x'}, dimensions={0} | all-to-all | bytes 196608 | tf_op jit(solution)/shard_map/all_to_all | solution.py:37
  289.0 4.7 %collective-permute-start.1 = (f32[24,128]{1,0:T(8,128)S(1)}, f32[24,128]{1,0:T(8,128)S(1)}, u32[]{:S(2)}, u32[]{:S(2)}) collective-permute-start(f32[24,128]{1,0:T(8,128)S(1)} %convert_reduce_fusion.1), channel_id=1, source_target_pairs={{0,1},{1,0},{2,3},{3,2},{4,5},{5,4},{6,7},{7,6},{8,9},{9,8},{10,11... | collective-permute-start | bytes 36872 | tf_op jit(solution)/shard_map/ppermute | solution.py:218
  293.7 0.8 collective-permute-done.1
  295.2 10.2 %all-to-all-start.10 = ((bf16[16,24,128]{2,1,0:T(8,128)(2,1)}), bf16[16,24,128]{2,1,0:T(8,128)(2,1)S(1)}, u32[]{:S(2)}, u32[]{:S(2)}) async-start(bf16[16,24,128]{2,1,0:T(8,128)(2,1)} %broadcast_in_dim.82), calls=%async_computation.10 | async-start | bytes 196608 | tf_op jit(solution)/shard_map/all_to_all | solution.py:37
  305.3 11.9 %all-to-all-done.10 = bf16[16,24,128]{2,1,0:T(8,128)(2,1)S(1)} async-done(((bf16[16,24,128]{2,1,0:T(8,128)(2,1)}), bf16[16,24,128]{2,1,0:T(8,128)(2,1)S(1)}, u32[]{:S(2)}, u32[]{:S(2)}) %all-to-all-start.10) | async-done | bytes 98336 | tf_op jit(solution)/shard_map/all_to_all | solution.py:37
  317.3 7.5 %all_to_all.76 = bf16[4,192,128]{2,1,0:T(8,128)(2,1)S(1)} all-to-all(bf16[4,192,128]{2,1,0:T(8,128)(2,1)S(1)} %broadcast_in_dim.83), channel_id=1, replica_groups=mesh['z'=16,'y'=4,'x'=4,'c'=2] {'y'}, dimensions={0} | all-to-all | bytes 393216 | tf_op jit(solution)/shard_map/all_to_all | solution.py:37
  324.8 1.0 broadcast_in_dim.84
  325.8 3.5 all-to-all-start.12
  329.4 1.5 gather_fusion
  330.9 6.8 %all-to-all-done.12 = bf16[4,4,192,128]{3,2,1,0:T(8,128)(2,1)S(1)} async-done(((bf16[4,4,192,128]{3,2,1,0:T(8,128)(2,1)}), bf16[4,4,192,128]{3,2,1,0:T(8,128)(2,1)S(1)}, u32[]{:S(2)}, u32[]{:S(2)}) %all-to-all-start.12) | async-done | bytes 786464 | tf_op jit(solution)/shard_map/all_to_all | solution.py:37
  337.7 7.0 %collective-permute-start.2 = (bf16[4,4,192,128]{3,2,1,0:T(8,128)(2,1)S(1)}, bf16[4,4,192,128]{3,2,1,0:T(8,128)(2,1)}, u32[]{:S(2)}, u32[]{:S(2)}) collective-permute-start(bf16[4,4,192,128]{3,2,1,0:T(8,128)(2,1)S(1)} %all-to-all-done.12), channel_id=1, source_target_pairs={{0,1},{1,0},{2,3},{3,2},{4,5},{5,4},{6,7},{7,6},{8,9},{9,8},{10,11... | collective-permute-start | bytes 2359304 | tf_op jit(solution)/shard_map/ppermute | solution.py:238
  345.1 1.7 fusion.6
  346.8 1.6 fusion.7
  348.4 1.2 select_bitcast_fusion.1
  350.1 1.9 convert_bitcast_fusion
  352.1 5.6 %copy.191 = f32[2,192,4,4,128]{4,3,2,1,0:T(4,128)} copy(f32[2,192,4,4,128]{4,1,2,3,0:T(8,128)} %convert_bitcast_fusion) | data formatting | bytes 6291456 | tf_op jit(solution)/shard_map/convert_element_type | solution.py:243
  357.6 5.1 %reshape.577 = f32[384,2048]{1,0:T(8,128)} reshape(f32[2,192,4,4,128]{4,3,2,1,0:T(4,128)} %copy.191) | data formatting | bytes 6291456 | tf_op jit(solution)/shard_map/convert_element_type | solution.py:243
  362.7 2.7 fusion.148
  366.2 3.6 all-to-all-start.13
  369.9 7.3 %all-to-all-done.13 = f32[32,3,128]{2,1,0:T(4,128)S(1)} async-done(((f32[32,3,128]{2,1,0:T(4,128)}), f32[32,3,128]{2,1,0:T(4,128)S(1)}, u32[]{:S(2)}, u32[]{:S(2)}) %all-to-all-start.13) | async-done | bytes 49184 | tf_op jit(solution)/shard_map/all_to_all | solution.py:37
  377.9 4.9 %all-to-all-start.14 = ((f32[16,3,128]{2,1,0:T(4,128)}), f32[16,3,128]{2,1,0:T(4,128)S(1)}, u32[]{:S(2)}, u32[]{:S(2)}) async-start(f32[16,3,128]{2,1,0:T(4,128)} %broadcast_in_dim.87), calls=%async_computation.14 | async-start | bytes 65536 | tf_op jit(solution)/shard_map/all_to_all | solution.py:37
  383.6 10.7 %all-to-all-done.14 = f32[16,3,128]{2,1,0:T(4,128)S(1)} async-done(((f32[16,3,128]{2,1,0:T(4,128)}), f32[16,3,128]{2,1,0:T(4,128)S(1)}, u32[]{:S(2)}, u32[]{:S(2)}) %all-to-all-start.14) | async-done | bytes 24608 | tf_op jit(solution)/shard_map/all_to_all | solution.py:37
  394.4 0.9 copy.196
  (196 shorter events, 18.0 us)
Async XLA Ops:
  0.6 362.1 %copy-start = (bf16[2048,256]{1,0:T(8,128)(2,1)S(1)}, bf16[2048,256]{1,0:T(8,128)(2,1)}, u32[]{:S(2)}) copy-start(bf16[2048,256]{1,0:T(8,128)(2,1)} %param.35) | copy-start | bytes 3145732
  0.6 16.4 %copy-start.18 = (s32[8,48]{1,0:T(8,128)S(1)}, s32[8,48]{1,0:T(8,128)}, u32[]{:S(2)}) copy-start(s32[8,48]{1,0:T(8,128)} %param.40) | copy-start | bytes 4612
  0.7 18.6 %copy-start.14 = (s32[8]{0:T(128)S(1)}, s32[8]{0:T(128)}, u32[]{:S(2)}) copy-start(s32[8]{0:T(128)} %param.39) | copy-start | bytes 100
  11.2 41.9 %copy-start.15 = (f32[128]{0:T(128)S(1)}, f32[128]{0:T(128)}, u32[]{:S(2)}) copy-start(f32[128]{0:T(128)} %param.27) | copy-start | bytes 1540
  11.2 42.2 %copy-start.16 = (f32[128]{0:T(128)S(1)}, f32[128]{0:T(128)}, u32[]{:S(2)}) copy-start(f32[128]{0:T(128)} %param.28) | copy-start | bytes 1540
  12.0 11.2 %all-to-all-start = ((bf16[4,32,1536]{2,1,0:T(8,128)(2,1)}), bf16[4,32,1536]{2,1,0:T(8,128)(2,1)S(1)}, u32[]{:S(2)}, u32[]{:S(2)}) async-start(bf16[4,32,1536]{2,1,0:T(8,128)(2,1)} %pad_maximum_fusion.1), calls=%async_computation | async-start | bytes 786432 | tf_op jit(solution)/shard_map/all_to_all | solution.py:37
  19.4 3.9 copy-start.9
  24.4 28.2 %all-to-all-start.1 = ((bf16[16,6,896]{2,1,0:T(8,128)(2,1)}), bf16[16,6,896]{2,1,0:T(8,128)(2,1)S(1)}, u32[]{:S(2)}, u32[]{:S(2)}) async-start(bf16[16,6,896]{2,1,0:T(8,128)(2,1)} %reshape.548), calls=%async_computation.1 | async-start | bytes 458752 | tf_op jit(solution)/shard_map/all_to_all | solution.py:37
  54.4 20.7 %all-to-all-start.2 = ((bf16[16,8,768]{2,1,0:T(8,128)(2,1)}), bf16[16,8,768]{2,1,0:T(8,128)(2,1)S(1)}, u32[]{:S(2)}, u32[]{:S(2)}) async-start(bf16[16,8,768]{2,1,0:T(8,128)(2,1)} %broadcast_in_dim.72), calls=%async_computation.2 | async-start | bytes 393216 | tf_op jit(solution)/shard_map/all_to_all | solution.py:37
  75.2 13.3 %copy-start.1 = (bf16[8,256,128]{2,1,0:T(8,128)(2,1)S(1)}, bf16[8,256,128]{2,1,0:T(8,128)(2,1)}, u32[]{:S(2)}) copy-start(bf16[8,256,128]{2,1,0:T(8,128)(2,1)} %param.37) | copy-start | bytes 1572868
  76.1 10.7 %all-to-all-start.3 = ((bf16[4,96,768]{2,1,0:T(8,128)(2,1)}), bf16[4,96,768]{2,1,0:T(8,128)(2,1)S(1)}, u32[]{:S(2)}, u32[]{:S(2)}) async-start(bf16[4,96,768]{2,1,0:T(8,128)(2,1)} %broadcast_in_dim.74), calls=%async_computation.3 | async-start | bytes 1179648 | tf_op jit(solution)/shard_map/all_to_all | solution.py:37
  79.5 0.6 copy-start.12
  87.3 3.3 copy-start.3
  88.0 3.1 copy-start.7
  88.1 3.1 copy-start.5
  88.1 2.5 copy-start.11
  92.5 19.8 %all-to-all-start.4 = ((bf16[16,56,128]{2,1,0:T(8,128)(2,1)}), bf16[16,56,128]{2,1,0:T(8,128)(2,1)S(1)}, u32[]{:S(2)}, u32[]{:S(2)}) async-start(bf16[16,56,128]{2,1,0:T(8,128)(2,1)} %fusion.36), calls=%async_computation.4 | async-start | bytes 458752 | tf_op jit(solution)/shard_map/all_to_all | solution.py:37
  113.5 8.3 %all-to-all-start.5 = ((bf16[4,152,128]{2,1,0:T(8,128)(2,1)}), bf16[4,152,128]{2,1,0:T(8,128)(2,1)S(1)}, u32[]{:S(2)}, u32[]{:S(2)}) async-start(bf16[4,152,128]{2,1,0:T(8,128)(2,1)} %broadcast_in_dim.80), calls=%async_computation.5 | async-start | bytes 311296 | tf_op jit(solution)/shard_map/all_to_all | solution.py:37
  123.6 121.9 %all-to-all-start.6 = ((bf16[16,128,640]{2,1,0:T(8,128)(2,1)}), bf16[16,128,640]{2,1,0:T(8,128)(2,1)}, u32[]{:S(2)}, u32[]{:S(2)}) async-start(bf16[16,128,640]{2,1,0:T(8,128)(2,1)} %stack.102), calls=%async_computation.6 | async-start | bytes 5242880 | tf_op jit(solution)/shard_map/all_to_all | solution.py:134
  247.6 11.4 %all-to-all-start.7 = ((bf16[16,24,128]{2,1,0:T(8,128)(2,1)}), bf16[16,24,128]{2,1,0:T(8,128)(2,1)S(1)}, u32[]{:S(2)}, u32[]{:S(2)}) async-start(bf16[16,24,128]{2,1,0:T(8,128)(2,1)} %bitcast.190), calls=%async_computation.7 | async-start | bytes 196608 | tf_op jit(solution)/shard_map/all_to_all | solution.py:37
  259.0 5.6 %collective-permute-start = (f32[24,128]{1,0:T(8,128)S(1)}, f32[24,128]{1,0:T(8,128)S(1)}, u32[]{:S(2)}, u32[]{:S(2)}) collective-permute-start(f32[24,128]{1,0:T(8,128)S(1)} %convert_reduce_fusion.2), channel_id=1, source_target_pairs={{0,1},{1,0},{2,3},{3,2},{4,5},{5,4},{6,7},{7,6},{8,9},{9,8},{10,11... | collective-permute-start | bytes 36872 | tf_op jit(solution)/shard_map/ppermute | solution.py:218
  265.3 10.1 %all-to-all-start.8 = ((bf16[16,24,128]{2,1,0:T(8,128)(2,1)}), bf16[16,24,128]{2,1,0:T(8,128)(2,1)S(1)}, u32[]{:S(2)}, u32[]{:S(2)}) async-start(bf16[16,24,128]{2,1,0:T(8,128)(2,1)} %broadcast_in_dim.81), calls=%async_computation.8 | async-start | bytes 196608 | tf_op jit(solution)/shard_map/all_to_all | solution.py:37
  277.4 52.0 %copy-start.19 = (s32[8]{0:T(128)S(1)}, s32[8]{0:T(128)}, u32[]{:S(2)}) copy-start(s32[8]{0:T(128)} %param.41) | copy-start | bytes 100
  277.4 67.3 %copy-start.10 = (s32[8,48]{1,0:T(8,128)S(1)}, s32[8,48]{1,0:T(8,128)}, u32[]{:S(2)}) copy-start(s32[8,48]{1,0:T(8,128)} %copy-done.9) | copy-start | bytes 4612
  277.4 67.3 %copy-start.13 = (s32[256]{0:T(256)S(1)}, s32[256]{0:T(256)}, u32[]{:S(2)}) copy-start(s32[256]{0:T(256)} %copy-done.12) | copy-start | bytes 3076
  277.4 67.5 %copy-start.17 = (f32[8]{0:T(128)S(1)}, f32[8]{0:T(128)}, u32[]{:S(2)}) copy-start(f32[8]{0:T(128)} %param.36) | copy-start | bytes 100
  277.4 67.7 %copy-start.2 = (bf16[8,256,128]{2,1,0:T(8,128)(2,1)S(1)}, bf16[8,256,128]{2,1,0:T(8,128)(2,1)}, u32[]{:S(2)}) copy-start(bf16[8,256,128]{2,1,0:T(8,128)(2,1)} %param.37) | copy-start | bytes 1572868
  277.4 67.7 %copy-start.8 = (bf16[384,128]{1,0:T(8,128)(2,1)S(1)}, bf16[384,128]{1,0:T(8,128)(2,1)}, u32[]{:S(2)}) copy-start(bf16[384,128]{1,0:T(8,128)(2,1)} %copy-done.7) | copy-start | bytes 294916
  289.0 57.8 %copy-start.4 = (bf16[8,256,128]{2,1,0:T(8,128)(2,1)S(1)}, bf16[8,256,128]{2,1,0:T(8,128)(2,1)}, u32[]{:S(2)}) copy-start(bf16[8,256,128]{2,1,0:T(8,128)(2,1)} %param.38) | copy-start | bytes 1572868
  289.0 57.8 %copy-start.6 = (bf16[384,128]{1,0:T(8,128)(2,1)S(1)}, bf16[384,128]{1,0:T(8,128)(2,1)}, u32[]{:S(2)}) copy-start(bf16[384,128]{1,0:T(8,128)(2,1)} %copy-done.5) | copy-start | bytes 294916
  289.0 5.5 %collective-permute-start.1 = (f32[24,128]{1,0:T(8,128)S(1)}, f32[24,128]{1,0:T(8,128)S(1)}, u32[]{:S(2)}, u32[]{:S(2)}) collective-permute-start(f32[24,128]{1,0:T(8,128)S(1)} %convert_reduce_fusion.1), channel_id=1, source_target_pairs={{0,1},{1,0},{2,3},{3,2},{4,5},{5,4},{6,7},{7,6},{8,9},{9,8},{10,11... | collective-permute-start | bytes 36872 | tf_op jit(solution)/shard_map/ppermute | solution.py:218
  295.2 22.1 %all-to-all-start.10 = ((bf16[16,24,128]{2,1,0:T(8,128)(2,1)}), bf16[16,24,128]{2,1,0:T(8,128)(2,1)S(1)}, u32[]{:S(2)}, u32[]{:S(2)}) async-start(bf16[16,24,128]{2,1,0:T(8,128)(2,1)} %broadcast_in_dim.82), calls=%async_computation.10 | async-start | bytes 196608 | tf_op jit(solution)/shard_map/all_to_all | solution.py:37
  325.8 11.8 %all-to-all-start.12 = ((bf16[4,4,192,128]{3,2,1,0:T(8,128)(2,1)}), bf16[4,4,192,128]{3,2,1,0:T(8,128)(2,1)S(1)}, u32[]{:S(2)}, u32[]{:S(2)}) async-start(bf16[4,4,192,128]{3,2,1,0:T(8,128)(2,1)} %broadcast_in_dim.84), calls=%async_computation.12 | async-start | bytes 1572864 | tf_op jit(solution)/shard_map/all_to_all | solution.py:37
  337.7 10.8 %collective-permute-start.2 = (bf16[4,4,192,128]{3,2,1,0:T(8,128)(2,1)S(1)}, bf16[4,4,192,128]{3,2,1,0:T(8,128)(2,1)}, u32[]{:S(2)}, u32[]{:S(2)}) collective-permute-start(bf16[4,4,192,128]{3,2,1,0:T(8,128)(2,1)S(1)} %all-to-all-done.12), channel_id=1, source_target_pairs={{0,1},{1,0},{2,3},{3,2},{4,5},{5,4},{6,7},{7,6},{8,9},{9,8},{10,11... | collective-permute-start | bytes 2359304 | tf_op jit(solution)/shard_map/ppermute | solution.py:238
  366.2 11.0 %all-to-all-start.13 = ((f32[32,3,128]{2,1,0:T(4,128)}), f32[32,3,128]{2,1,0:T(4,128)S(1)}, u32[]{:S(2)}, u32[]{:S(2)}) async-start(f32[32,3,128]{2,1,0:T(4,128)} %broadcast_in_dim.86), calls=%async_computation.13 | async-start | bytes 131072 | tf_op jit(solution)/shard_map/all_to_all | solution.py:37
  377.9 16.4 %all-to-all-start.14 = ((f32[16,3,128]{2,1,0:T(4,128)}), f32[16,3,128]{2,1,0:T(4,128)S(1)}, u32[]{:S(2)}, u32[]{:S(2)}) async-start(f32[16,3,128]{2,1,0:T(4,128)} %broadcast_in_dim.87), calls=%async_computation.14 | async-start | bytes 65536 | tf_op jit(solution)/shard_map/all_to_all | solution.py:37
